TPU v7x, 32 devices: a whole 2x2x4 slice. The times are simulated.
32 devices in a mesh: sec: 4 (over x, core), sub: 8 (over z, y).
Axes of the slice: x: 2, y: 2, z: 4, core: 2. Of those that a mesh axis runs over, the one named last changes fastest.
Arguments:
- schur: bfloat16 [8, 1024, 1024], P('sub', 'sec'), may hold values from -0.1875 to 0.1875
- neumann: bfloat16 [8, 1024, 1024], P('sub', 'sec'), may hold values from -0.1875 to 0.1875
- constraint_weights: bfloat16 [8, 1024, 128], P('sub', 'sec'), may hold values from -0.1875 to 0.1875
- coarse_inverse: bfloat16 [8, 768, 768], P('sub', 'sec'), may hold values from -0.21875 to 0.21875
- solution: bfloat16 [8, 1024, 128], P('sub', 'sec'), may hold values from -6 to 6
- load: bfloat16 [8, 1024, 128], P('sub', 'sec'), may hold values from -6 to 6
- neighbours: int32 [8, 4], P('sub'), may hold values from 0 to 7, as said below
- face_index: int32 [8, 1024], P('sub', 'sec'), may hold values from 0 to 255, as said below
- coarse_dof: int32 [8, 128], P('sub'), may hold values from 0 to 6143, as said below
Outputs:
- precond: bfloat16 [8, 1024, 128], P('sub', 'sec')
- image: bfloat16 [8, 1024, 128], P('sub', 'sec')
Inputs may be any that keep to these rules, and one draw needn't show every extreme that they name: `neighbours`: the subdomain glued to face f of subdomain i is another subdomain whose column c // 1 is the column i // 1 of i or the one before or after it, cyclically over 8 columns. `face_index`: for each subdomain and face, the entries of the face's 256 unknowns are a permutation of 0 to 255. `coarse_dof`: constraint k of subdomain i maps to an unknown of the cluster of column i // 1 or of the column before or after it, cyclically. Each cluster has 64 coarse unknowns that are used, and each used unknown is the unknown of exactly two constraints.
All inputs are finite; a program needn't handle non-finite values.
Results may differ from a plain program's by a relative error of at most 0.0058.
Values may be sent and summed in bfloat16 or wider, within the bound.
No kernel may reach another device: no remote copies, remote signals or barrier semaphores. Data moves between devices by JAX's collectives and lax.ppermute only.
A program may use at most 64 MiB of HBM per device.

v0:
```python
import jax
import jax.numpy as jnp
from jax import lax
from jax.sharding import PartitionSpec as P

COLS = 128


def extended(cells, sides, width):
    for axis, dim in sides:
        count = lax.axis_size(axis)
        head = lax.slice_in_dim(cells, 0, width, axis=dim)
        tail = lax.slice_in_dim(cells, cells.shape[dim] - width, cells.shape[dim], axis=dim)
        cells = jnp.concatenate(
            [
                lax.ppermute(tail, axis, [(i, (i + 1) % count) for i in range(count)]),
                cells,
                lax.ppermute(head, axis, [((i + 1) % count, i) for i in range(count)]),
            ],
            axis=dim,
        )
    return cells


def row_folder(blocks, received):
    return jnp.einsum("srk,skc->src", blocks, received, preferred_element_type=jnp.float32)


def face_selector(face_index):
    face_len = face_index.shape[1]
    positions = lax.broadcasted_iota(jnp.int32, (face_index.shape[0], face_len, face_len), 2)
    return (face_index[:, :, None] == positions).astype(jnp.float32)


def pair_faces(own_field, rim_rows, rim_slot, selector):
    matched = jnp.take(rim_rows, rim_slot, axis=0)
    facing = jnp.einsum(
        "sde,sec->sdc",
        selector,
        matched,
        precision=lax.Precision.HIGHEST,
        preferred_element_type=jnp.float32,
    )
    return own_field + facing


def local(
    schur,
    neumann,
    constraint_weights,
    coarse_inverse,
    solution,
    load,
    neighbours,
    face_index,
    coarse_dof,
):
    sub_count = schur.shape[0]
    col_count = COLS
    coarse_len = coarse_inverse.shape[2]
    inverse_rows = coarse_inverse[0]
    my_column = lax.axis_index("sub")
    axis_len = lax.axis_size("sub")
    my_section = lax.axis_index("sec")
    nbr_ids = jnp.take(neighbours, my_section, axis=1)
    rim_slot = (nbr_ids // sub_count - my_column + 1) % axis_len * sub_count + nbr_ids % sub_count
    coarse_slot = (
        coarse_dof // coarse_len - my_column + 1
    ) % axis_len * coarse_len + coarse_dof % coarse_len
    selector = face_selector(face_index)
    dof_near = extended(coarse_dof, (("sub", 0),), sub_count)
    is_owned = dof_near // coarse_len == my_column
    owned_slot = jnp.where(is_owned, dof_near % coarse_len, coarse_len).reshape(-1)
    schur_iter = row_folder(schur, lax.all_gather(solution, "sec", axis=1, tiled=True))
    residual = load.astype(jnp.float32) - schur_iter
    residual_near = extended(residual, (("sub", 0),), sub_count)
    assembled = pair_faces(residual, residual_near, rim_slot, selector).astype(jnp.bfloat16)
    constraint_part = jnp.einsum(
        "srk,src->skc", constraint_weights, assembled, preferred_element_type=jnp.float32
    )
    constraint_values = lax.psum(constraint_part, "sec")
    value_near = extended(constraint_values, (("sub", 0),), sub_count)
    coarse_rhs = jax.ops.segment_sum(
        value_near.reshape(-1, col_count), owned_slot, num_segments=coarse_len + 1
    )[:coarse_len]
    coarse_piece = jnp.dot(
        inverse_rows, coarse_rhs.astype(jnp.bfloat16), preferred_element_type=jnp.float32
    ).astype(jnp.bfloat16)
    coarse_whole = lax.all_gather(coarse_piece, "sec", axis=0, tiled=True)
    coarse_near = extended(coarse_whole, (("sub", 0),), coarse_len)
    picked = jnp.take(coarse_near, coarse_slot.reshape(-1), axis=0).reshape(
        sub_count, -1, col_count
    )
    neumann_part = row_folder(neumann, lax.all_gather(assembled, "sec", axis=1, tiled=True))
    correction = neumann_part + jnp.einsum(
        "srk,skc->src", constraint_weights, picked, preferred_element_type=jnp.float32
    )
    correction_near = extended(correction, (("sub", 0),), sub_count)
    precond = (0.5 * pair_faces(correction, correction_near, rim_slot, selector)).astype(
        jnp.bfloat16
    )
    precond_image = row_folder(schur, lax.all_gather(precond, "sec", axis=1, tiled=True)).astype(
        jnp.bfloat16
    )
    return (precond, precond_image)


def solution(mesh):
    placed = (
        P("sub", "sec", None),
        P("sub", "sec", None),
        P("sub", "sec", None),
        P("sub", "sec", None),
        P("sub", "sec", None),
        P("sub", "sec", None),
        P("sub", None),
        P("sub", "sec"),
        P("sub", None),
    )
    return jax.shard_map(
        local,
        mesh=mesh,
        in_specs=placed,
        out_specs=(P("sub", "sec", None), P("sub", "sec", None)),
        check_vma=False,
    )
```

profile of v0, /device:TPU:0, one launch (start us, length us, event | category | flops | bytes accessed | tf_op | source)
XLA Modules:
  0.0 114.4 jit_solution(5369333689216355976)
XLA Ops:
  7.2 7.6 %all_gather.12 = bf16[1,1024,128]{2,1,0:T(8,128)(2,1)S(1)} all-gather(bf16[1,256,128]{2,1,0:T(8,128)(2,1)} %param.15), channel_id=1, replica_groups=mesh['sec'=4,'sub'=8] {'sec'}, dimensions={1}, use_global_device_ids=true | all-gather | bytes 327680 | tf_op jit(solution)/shard_map/all_gather | solution.py:74
  14.8 1.2 %fusion.2 = f32[1,256,128]{2,1,0:T(8,128)S(1)} fusion(bf16[1,256,1024]{2,1,0:T(8,128)(2,1)S(1)} %copy-done, bf16[1,1024,128]{2,1,0:T(8,128)(2,1)S(1)} %all_gather.12, bf16[1,256,128]{2,1,0:T(8,128)(2,1)} %param.16), kind=kOutput, calls=%fused_computation.8 | convolution fusion | flops 67174400 | bytes 983040 | tf_op jit(solution)/shard_map/srk,skc->src/dot_general | solution.py:26
  16.0 1.6 %collective-permute-start = (f32[1,256,128]{2,1,0:T(8,128)S(1)}, f32[1,256,128]{2,1,0:T(8,128)S(1)}, u32[]{:S(2)}, u32[]{:S(2)}) collective-permute-start(f32[1,256,128]{2,1,0:T(8,128)S(1)} %fusion.2), channel_id=1, source_target_pairs={{0,1},{1,2},{2,3},{3,4},{4,5},{5,6},{6,7},{7,0},{8,9},{9,10},{10,1... | collective-permute-start | bytes 393224 | tf_op jit(solution)/shard_map/ppermute | solution.py:16
  17.6 3.2 %collective-permute-start.1 = (f32[1,256,128]{2,1,0:T(8,128)S(1)}, f32[1,256,128]{2,1,0:T(8,128)S(1)}, u32[]{:S(2)}, u32[]{:S(2)}) collective-permute-start(f32[1,256,128]{2,1,0:T(8,128)S(1)} %fusion.2), channel_id=1, source_target_pairs={{1,0},{2,1},{3,2},{4,3},{5,4},{6,5},{7,6},{0,7},{9,8},{10,9},{11,1... | collective-permute-start | bytes 393224 | tf_op jit(solution)/shard_map/ppermute | solution.py:18
  20.8 4.7 %collective-permute-start.3 = (s32[1,128]{1,0:T(1,128)S(1)}, s32[1,128]{1,0:T(1,128)S(1)}, u32[]{:S(2)}, u32[]{:S(2)}) collective-permute-start(s32[1,128]{1,0:T(1,128)S(1)} %copy-done.4), channel_id=1, source_target_pairs={{1,0},{2,1},{3,2},{4,3},{5,4},{6,5},{7,6},{0,7},{9,8},{10,9},{11,1... | collective-permute-start | bytes 1544 | tf_op jit(solution)/shard_map/ppermute | solution.py:18
  25.5 0.6 constant_dynamic-slice_fusion
  27.4 0.8 convolution_bitcast_fusion.2
  28.3 33.1 %all-reduce.2.cloned.1.call-done = f32[1,128,128]{1,2,0:T(8,128)} async-done(((f32[1,128,128]{1,2,0:T(8,128)}), f32[1,128,128]{1,2,0:T(8,128)}) %all-reduce.2.cloned.1.call-update) | async-done | bytes 65552 | tf_op jit(solution)/shard_map/psum | solution.py:81
  61.4 1.5 %collective-permute-start.4 = (f32[1,128,128]{1,2,0:T(8,128)}, f32[1,128,128]{1,2,0:T(8,128)S(1)}, u32[]{:S(2)}, u32[]{:S(2)}) collective-permute-start(f32[1,128,128]{1,2,0:T(8,128)} %all-reduce.2.cloned.1.call-done), channel_id=1, source_target_pairs={{0,1},{1,2},{2,3},{3,4},{4,5},{5,6},{6,7},{7,0},{8,9},{9,10},{10,1... | collective-permute-start | bytes 196616 | tf_op jit(solution)/shard_map/ppermute | solution.py:16
  62.9 3.2 %collective-permute-start.5 = (f32[1,128,128]{1,2,0:T(8,128)}, f32[1,128,128]{1,2,0:T(8,128)S(1)}, u32[]{:S(2)}, u32[]{:S(2)}) collective-permute-start(f32[1,128,128]{1,2,0:T(8,128)} %all-reduce.2.cloned.1.call-done), channel_id=1, source_target_pairs={{1,0},{2,1},{3,2},{4,3},{5,4},{6,5},{7,6},{0,7},{9,8},{10,9},{11,1... | collective-permute-start | bytes 196616 | tf_op jit(solution)/shard_map/ppermute | solution.py:18
  66.2 2.4 %collective-permute-done.4 = f32[1,128,128]{1,2,0:T(8,128)S(1)} collective-permute-done((f32[1,128,128]{1,2,0:T(8,128)}, f32[1,128,128]{1,2,0:T(8,128)S(1)}, u32[]{:S(2)}, u32[]{:S(2)}) %collective-permute-start.4) | collective-permute-done | bytes 65568 | tf_op jit(solution)/shard_map/ppermute | solution.py:16
  68.6 0.9 pad_maximum_fusion.1
  69.6 2.5 %scatter_custom_fusion = f32[769,128]{1,0:T(8,128)S(1)} fusion(s32[384]{0:T(512)S(1)} %fusion.45, f32[384,128]{1,0:T(8,128)S(1)} %bitcast.118, f32[]{:T(128)} %constant.133.clone.1), kind=kCustom, calls=%fused_computation.32 | custom fusion | flops 49152 | bytes 393732 | tf_op jit(solution)/shard_map/scatter-add | solution.py:83
  72.3 5.6 %all_gather.14 = bf16[768,128]{1,0:T(8,128)(2,1)S(1)} all-gather(bf16[192,128]{1,0:T(8,128)(2,1)S(1)} %fusion.6), channel_id=1, replica_groups=mesh['sec'=4,'sub'=8] {'sec'}, dimensions={0}, use_global_device_ids=true | all-gather | bytes 245760 | tf_op jit(solution)/shard_map/all_gather | solution.py:89
  77.9 1.1 collective-permute-start.6
  79.0 3.6 %collective-permute-start.7 = (bf16[768,128]{1,0:T(8,128)(2,1)S(1)}, bf16[768,128]{1,0:T(8,128)(2,1)S(1)}, u32[]{:S(2)}, u32[]{:S(2)}) collective-permute-start(bf16[768,128]{1,0:T(8,128)(2,1)S(1)} %all_gather.14), channel_id=1, source_target_pairs={{1,0},{2,1},{3,2},{4,3},{5,4},{6,5},{7,6},{0,7},{9,8},{10,9},{11,1... | collective-permute-start | bytes 589832 | tf_op jit(solution)/shard_map/ppermute | solution.py:18
  82.6 5.8 %all_gather.13 = bf16[1,1024,128]{2,1,0:T(8,128)(2,1)S(1)} all-gather(bf16[1,256,128]{2,1,0:T(8,128)(2,1)S(1)} %fusion.4), channel_id=1, replica_groups=mesh['sec'=4,'sub'=8] {'sec'}, dimensions={1}, use_global_device_ids=true | all-gather | bytes 327680 | tf_op jit(solution)/shard_map/all_gather | solution.py:94
  88.4 1.7 %collective-permute-done.7 = bf16[768,128]{1,0:T(8,128)(2,1)S(1)} collective-permute-done((bf16[768,128]{1,0:T(8,128)(2,1)S(1)}, bf16[768,128]{1,0:T(8,128)(2,1)S(1)}, u32[]{:S(2)}, u32[]{:S(2)}) %collective-permute-start.7) | collective-permute-done | bytes 196640 | tf_op jit(solution)/shard_map/ppermute | solution.py:18
  90.1 0.7 gather_fusion
  91.8 4.4 %collective-permute-start.9 = (f32[1,256,128]{1,2,0:T(8,128)S(1)}, f32[1,256,128]{1,2,0:T(8,128)S(1)}, u32[]{:S(2)}, u32[]{:S(2)}) collective-permute-start(f32[1,256,128]{1,2,0:T(8,128)S(1)} %bitcast.115), channel_id=1, source_target_pairs={{1,0},{2,1},{3,2},{4,3},{5,4},{6,5},{7,6},{0,7},{9,8},{10,9},{11,1... | collective-permute-start | bytes 393224 | tf_op jit(solution)/shard_map/ppermute | solution.py:18
  96.2 2.9 %collective-permute-done.8 = f32[1,256,128]{1,2,0:T(8,128)S(1)} collective-permute-done((f32[1,256,128]{1,2,0:T(8,128)S(1)}, f32[1,256,128]{1,2,0:T(8,128)S(1)}, u32[]{:S(2)}, u32[]{:S(2)}) %collective-permute-start.8) | collective-permute-done | bytes 131104 | tf_op jit(solution)/shard_map/ppermute | solution.py:16
  100.0 5.8 %all-gather = bf16[1024,128]{0,1:T(8,128)(2,1)S(1)} all-gather(bf16[256,128]{0,1:T(8,128)(2,1)S(1)} %fusion.3), channel_id=2, replica_groups=mesh['sec'=4,'sub'=8] {'sec'}, dimensions={0}, use_global_device_ids=true | all-gather | bytes 327680 | tf_op jit(solution)/shard_map/all_gather | solution.py:102
  106.1 0.7 copy.17
  106.8 0.7 copy.16
  (39 shorter events, 3.1 us)
Async XLA Ops:
  7.2 7.6 %copy-start = (bf16[1,256,1024]{2,1,0:T(8,128)(2,1)S(1)}, bf16[1,256,1024]{2,1,0:T(8,128)(2,1)}, u32[]{:S(2)}) copy-start(bf16[1,256,1024]{2,1,0:T(8,128)(2,1)} %param.11) | copy-start | bytes 1572868
  7.2 13.6 %copy-start.4 = (s32[1,128]{1,0:T(1,128)S(1)}, s32[1,128]{1,0:T(1,128)}, u32[]{:S(2)}) copy-start(s32[1,128]{1,0:T(1,128)} %param.19) | copy-start | bytes 1540
  7.2 18.3 %copy-start.6 = (s32[1,4]{1,0:T(1,128)S(1)}, s32[1,4]{1,0:T(1,128)}, u32[]{:S(2)}) copy-start(s32[1,4]{1,0:T(1,128)} %param.17) | copy-start | bytes 52
  7.2 54.2 %all-reduce.2.cloned.1.call-start = ((), (), s32[]{:S(2)}) async-start(), calls=%async_computation | async-start | bytes 131072 | tf_op jit(solution)/shard_map/psum | solution.py:81
  14.8 12.3 %copy-start.5 = (s32[1,256]{1,0:T(1,128)S(1)}, s32[1,256]{1,0:T(1,128)}, u32[]{:S(2)}) copy-start(s32[1,256]{1,0:T(1,128)} %param.18) | copy-start | bytes 3076
  14.8 12.6 %copy-start.3 = (bf16[1,256,128]{2,1,0:T(8,128)(2,1)S(1)}, bf16[1,256,128]{2,1,0:T(8,128)(2,1)}, u32[]{:S(2)}) copy-start(bf16[1,256,128]{2,1,0:T(8,128)(2,1)} %param.13) | copy-start | bytes 196612
  16.0 11.1 %collective-permute-start = (f32[1,256,128]{2,1,0:T(8,128)S(1)}, f32[1,256,128]{2,1,0:T(8,128)S(1)}, u32[]{:S(2)}, u32[]{:S(2)}) collective-permute-start(f32[1,256,128]{2,1,0:T(8,128)S(1)} %fusion.2), channel_id=1, source_target_pairs={{0,1},{1,2},{2,3},{3,4},{4,5},{5,6},{6,7},{7,0},{8,9},{9,10},{10,1... | collective-permute-start | bytes 393224 | tf_op jit(solution)/shard_map/ppermute | solution.py:16
  17.6 9.5 %collective-permute-start.1 = (f32[1,256,128]{2,1,0:T(8,128)S(1)}, f32[1,256,128]{2,1,0:T(8,128)S(1)}, u32[]{:S(2)}, u32[]{:S(2)}) collective-permute-start(f32[1,256,128]{2,1,0:T(8,128)S(1)} %fusion.2), channel_id=1, source_target_pairs={{1,0},{2,1},{3,2},{4,3},{5,4},{6,5},{7,6},{0,7},{9,8},{10,9},{11,1... | collective-permute-start | bytes 393224 | tf_op jit(solution)/shard_map/ppermute | solution.py:18
  20.8 6.3 %collective-permute-start.2 = (s32[1,128]{1,0:T(1,128)S(1)}, s32[1,128]{1,0:T(1,128)S(1)}, u32[]{:S(2)}, u32[]{:S(2)}) collective-permute-start(s32[1,128]{1,0:T(1,128)S(1)} %copy-done.4), channel_id=1, source_target_pairs={{0,1},{1,2},{2,3},{3,4},{4,5},{5,6},{6,7},{7,0},{8,9},{9,10},{10,1... | collective-permute-start | bytes 1544 | tf_op jit(solution)/shard_map/ppermute | solution.py:16
  20.8 6.3 %collective-permute-start.3 = (s32[1,128]{1,0:T(1,128)S(1)}, s32[1,128]{1,0:T(1,128)S(1)}, u32[]{:S(2)}, u32[]{:S(2)}) collective-permute-start(s32[1,128]{1,0:T(1,128)S(1)} %copy-done.4), channel_id=1, source_target_pairs={{1,0},{2,1},{3,2},{4,3},{5,4},{6,5},{7,6},{0,7},{9,8},{10,9},{11,1... | collective-permute-start | bytes 1544 | tf_op jit(solution)/shard_map/ppermute | solution.py:18
  61.4 7.2 %collective-permute-start.4 = (f32[1,128,128]{1,2,0:T(8,128)}, f32[1,128,128]{1,2,0:T(8,128)S(1)}, u32[]{:S(2)}, u32[]{:S(2)}) collective-permute-start(f32[1,128,128]{1,2,0:T(8,128)} %all-reduce.2.cloned.1.call-done), channel_id=1, source_target_pairs={{0,1},{1,2},{2,3},{3,4},{4,5},{5,6},{6,7},{7,0},{8,9},{9,10},{10,1... | collective-permute-start | bytes 196616 | tf_op jit(solution)/shard_map/ppermute | solution.py:16
  62.9 5.7 %collective-permute-start.5 = (f32[1,128,128]{1,2,0:T(8,128)}, f32[1,128,128]{1,2,0:T(8,128)S(1)}, u32[]{:S(2)}, u32[]{:S(2)}) collective-permute-start(f32[1,128,128]{1,2,0:T(8,128)} %all-reduce.2.cloned.1.call-done), channel_id=1, source_target_pairs={{1,0},{2,1},{3,2},{4,3},{5,4},{6,5},{7,6},{0,7},{9,8},{10,9},{11,1... | collective-permute-start | bytes 196616 | tf_op jit(solution)/shard_map/ppermute | solution.py:18
  66.1 5.9 %copy-start.2 = (bf16[1,192,768]{2,1,0:T(8,128)(2,1)S(1)}, bf16[1,192,768]{2,1,0:T(8,128)(2,1)}, u32[]{:S(2)}) copy-start(bf16[1,192,768]{2,1,0:T(8,128)(2,1)} %param.14) | copy-start | bytes 884740
  77.9 10.5 %collective-permute-start.6 = (bf16[768,128]{1,0:T(8,128)(2,1)S(1)}, bf16[768,128]{1,0:T(8,128)(2,1)S(1)}, u32[]{:S(2)}, u32[]{:S(2)}) collective-permute-start(bf16[768,128]{1,0:T(8,128)(2,1)S(1)} %all_gather.14), channel_id=1, source_target_pairs={{0,1},{1,2},{2,3},{3,4},{4,5},{5,6},{6,7},{7,0},{8,9},{9,10},{10,1... | collective-permute-start | bytes 589832 | tf_op jit(solution)/shard_map/ppermute | solution.py:16
  79.0 11.1 %collective-permute-start.7 = (bf16[768,128]{1,0:T(8,128)(2,1)S(1)}, bf16[768,128]{1,0:T(8,128)(2,1)S(1)}, u32[]{:S(2)}, u32[]{:S(2)}) collective-permute-start(bf16[768,128]{1,0:T(8,128)(2,1)S(1)} %all_gather.14), channel_id=1, source_target_pairs={{1,0},{2,1},{3,2},{4,3},{5,4},{6,5},{7,6},{0,7},{9,8},{10,9},{11,1... | collective-permute-start | bytes 589832 | tf_op jit(solution)/shard_map/ppermute | solution.py:18
  88.4 2.7 %copy-start.1 = (bf16[1,256,1024]{2,1,0:T(8,128)(2,1)S(1)}, bf16[1,256,1024]{2,1,0:T(8,128)(2,1)}, u32[]{:S(2)}) copy-start(bf16[1,256,1024]{2,1,0:T(8,128)(2,1)} %param.12) | copy-start | bytes 1572868
  91.4 7.7 %collective-permute-start.8 = (f32[1,256,128]{1,2,0:T(8,128)S(1)}, f32[1,256,128]{1,2,0:T(8,128)S(1)}, u32[]{:S(2)}, u32[]{:S(2)}) collective-permute-start(f32[1,256,128]{1,2,0:T(8,128)S(1)} %bitcast.114), channel_id=1, source_target_pairs={{0,1},{1,2},{2,3},{3,4},{4,5},{5,6},{6,7},{7,0},{8,9},{9,10},{10,1... | collective-permute-start | bytes 393224 | tf_op jit(solution)/shard_map/ppermute | solution.py:16
  91.8 7.8 %collective-permute-start.9 = (f32[1,256,128]{1,2,0:T(8,128)S(1)}, f32[1,256,128]{1,2,0:T(8,128)S(1)}, u32[]{:S(2)}, u32[]{:S(2)}) collective-permute-start(f32[1,256,128]{1,2,0:T(8,128)S(1)} %bitcast.115), channel_id=1, source_target_pairs={{1,0},{2,1},{3,2},{4,3},{5,4},{6,5},{7,6},{0,7},{9,8},{10,9},{11,1... | collective-permute-start | bytes 393224 | tf_op jit(solution)/shard_map/ppermute | solution.py:18
Sparse Core Ops, SparseCore 0:
  28.4 32.9 all-reduce.1
where the time goes:
time: 115 us; the launch traced here: 114 us
  waiting for transfers between devices  40.9 us (36%)
  blocking collectives  24.7 us (21%)
  starting transfers between devices  23.8 us (21%)
  between operations  14.9 us (13%)
  matrix products  3.78 us (3%)
  other arithmetic  3.45 us (3%)
  local copies, waits for them, and re-layouts  2.92 us (3%)
    psum x1, waiting for transfers between devices, local(): constraint_values = lax.psum(constraint_part, 'sec')  33.1 us
    ppermute x5, starting transfers between devices, extended(): lax.ppermute(head, axis, [((i + 1) % count, i) for i in range(count)])  19.2 us
    all_gather x1, blocking collectives, local(): lax.all_gather(solution, 'sec', axis=1, tiled=True)  7.57 us
    all_gather x1, blocking collectives, local(): lax.all_gather(precond, 'sec', axis=1, tiled=True)  5.78 us
    all_gather x1, blocking collectives, local(): lax.all_gather(assembled, 'sec', axis=1, tiled=True)  5.76 us
    all_gather x1, blocking collectives, local(): coarse_whole = lax.all_gather(coarse_piece, 'sec', axis=0, tiled=True)  5.6 us
    ppermute x5, waiting for transfers between devices, extended(): lax.ppermute(tail, axis, [(i, (i + 1) % count) for i in range(count)])  5.58 us
    ppermute x5, starting transfers between devices, extended(): lax.ppermute(tail, axis, [(i, (i + 1) % count) for i in range(count)])  4.55 us
  transfers between devices with their start and end apart: 11, of which 6 were waited for; matrix products, arithmetic and copies ran while one was open for 1% of the time, Pallas kernels for 0%

commit v1 on v0

--- a/solution.py
+++ b/solution.py
@@ -78,7 +78,8 @@
     constraint_part = jnp.einsum(
         "srk,src->skc", constraint_weights, assembled, preferred_element_type=jnp.float32
     )
-    constraint_values = lax.psum(constraint_part, "sec")
+    parts = lax.all_gather(constraint_part, "sec")
+    constraint_values = jnp.sum(parts, axis=0)
     value_near = extended(constraint_values, (("sub", 0),), sub_count)
     coarse_rhs = jax.ops.segment_sum(
         value_near.reshape(-1, col_count), owned_slot, num_segments=coarse_len + 1

time: 115 us -> 71.9 us (0.63)
  waiting for transfers between devices: 40.9 us -> 6.95 us
  between operations: 14.9 us -> 1.51 us
  blocking collectives: 24.7 us -> 30.5 us
    psum x1 -> x0, waiting for transfers between devices: 33.1 us -> none  [local(): constraint_values = lax.psum(constraint_part, 'sec')]
    all_gather x0 -> x1, blocking collectives: none -> 5.78 us  [local(): parts = lax.all_gather(constraint_part, 'sec')]
    ppermute x5, starting transfers between devices: 19.2 us -> 21.8 us  [extended(): lax.ppermute(head, axis, [((i + 1) % count, i) for i in range(count)])]
    ppermute x5, starting transfers between devices: 4.55 us -> 2 us  [extended(): lax.ppermute(tail, axis, [(i, (i + 1) % count) for i in range(count)])]
  transfers between devices with their start and end apart: 11 -> 10, of which waited for: 6 -> 5; matrix products, arithmetic and copies ran while one was open for 1% -> 1% of each run, Pallas kernels for 0% -> 0%
where the time goes in v1:
time: 71.9 us; the launch traced here: 71.7 us
  blocking collectives  30.5 us (42%)
  starting transfers between devices  23.8 us (33%)
  waiting for transfers between devices  6.95 us (10%)
  matrix products  3.14 us (4%)
  local copies, waits for them, and re-layouts  3.01 us (4%)
  other arithmetic  2.77 us (4%)
  between operations  1.51 us (2%)
    ppermute x5, starting transfers between devices, extended(): lax.ppermute(head, axis, [((i + 1) % count, i) for i in range(count)])  21.8 us
    all_gather x1, blocking collectives, local(): lax.all_gather(solution, 'sec', axis=1, tiled=True)  7.57 us
    all_gather x1, blocking collectives, local(): parts = lax.all_gather(constraint_part, 'sec')  5.78 us
    all_gather x1, blocking collectives, local(): lax.all_gather(precond, 'sec', axis=1, tiled=True)  5.78 us
    ppermute x5, waiting for transfers between devices, extended(): lax.ppermute(tail, axis, [(i, (i + 1) % count) for i in range(count)])  5.77 us
    all_gather x1, blocking collectives, local(): lax.all_gather(assembled, 'sec', axis=1, tiled=True)  5.76 us
    all_gather x1, blocking collectives, local(): coarse_whole = lax.all_gather(coarse_piece, 'sec', axis=0, tiled=True)  5.6 us
    scatter-add x1, other arithmetic, local(): jax.ops.segment_sum(value_near.reshape(-1, col_count), owned_slot, num_se...  2.46 us
  transfers between devices with their start and end apart: 10, of which 5 were waited for; matrix products, arithmetic and copies ran while one was open for 1% of the time, Pallas kernels for 0%

profile of v1, /device:TPU:0, one launch (start us, length us, event | category | flops | bytes accessed | tf_op | source)
XLA Modules:
  0.0 71.7 jit_solution(14184764025865215763)
XLA Ops:
  0.7 7.6 %all_gather.18 = bf16[1,1024,128]{2,1,0:T(8,128)(2,1)S(1)} all-gather(bf16[1,256,128]{2,1,0:T(8,128)(2,1)} %param.15), channel_id=1, replica_groups=mesh['sec'=4,'sub'=8] {'sec'}, dimensions={1}, use_global_device_ids=true | all-gather | bytes 327680 | tf_op jit(solution)/shard_map/all_gather | solution.py:74
  8.2 1.2 %fusion.2 = f32[1,256,128]{2,1,0:T(8,128)S(1)} fusion(bf16[1,256,1024]{2,1,0:T(8,128)(2,1)S(1)} %copy-done, bf16[1,1024,128]{2,1,0:T(8,128)(2,1)S(1)} %all_gather.18, bf16[1,256,128]{2,1,0:T(8,128)(2,1)} %param.16), kind=kOutput, calls=%fused_computation.8 | convolution fusion | flops 67174400 | bytes 983040 | tf_op jit(solution)/shard_map/srk,skc->src/dot_general | solution.py:26
  9.4 1.6 %collective-permute-start = (f32[1,256,128]{2,1,0:T(8,128)S(1)}, f32[1,256,128]{2,1,0:T(8,128)S(1)}, u32[]{:S(2)}, u32[]{:S(2)}) collective-permute-start(f32[1,256,128]{2,1,0:T(8,128)S(1)} %fusion.2), channel_id=1, source_target_pairs={{0,1},{1,2},{2,3},{3,4},{4,5},{5,6},{6,7},{7,0},{8,9},{9,10},{10,1... | collective-permute-start | bytes 393224 | tf_op jit(solution)/shard_map/ppermute | solution.py:16
  11.0 3.2 %collective-permute-start.1 = (f32[1,256,128]{2,1,0:T(8,128)S(1)}, f32[1,256,128]{2,1,0:T(8,128)S(1)}, u32[]{:S(2)}, u32[]{:S(2)}) collective-permute-start(f32[1,256,128]{2,1,0:T(8,128)S(1)} %fusion.2), channel_id=1, source_target_pairs={{1,0},{2,1},{3,2},{4,3},{5,4},{6,5},{7,6},{0,7},{9,8},{10,9},{11,1... | collective-permute-start | bytes 393224 | tf_op jit(solution)/shard_map/ppermute | solution.py:18
  14.2 4.7 %collective-permute-start.3 = (s32[1,128]{1,0:T(1,128)S(1)}, s32[1,128]{1,0:T(1,128)S(1)}, u32[]{:S(2)}, u32[]{:S(2)}) collective-permute-start(s32[1,128]{1,0:T(1,128)S(1)} %copy-done.4), channel_id=1, source_target_pairs={{1,0},{2,1},{3,2},{4,3},{5,4},{6,5},{7,6},{0,7},{9,8},{10,9},{11,1... | collective-permute-start | bytes 1544 | tf_op jit(solution)/shard_map/ppermute | solution.py:18
  18.9 0.6 constant_dynamic-slice_fusion
  21.0 5.8 %all-gather = f32[512,128]{0,1:T(8,128)S(1)} all-gather(f32[128,128]{0,1:T(8,128)S(1)} %convolution_bitcast_fusion.2), channel_id=2, replica_groups=mesh['sec'=4,'sub'=8] {'sec'}, dimensions={0}, use_global_device_ids=true | all-gather | bytes 327680 | tf_op jit(solution)/shard_map/all_gather | solution.py:81
  27.1 4.8 %collective-permute-start.5 = (f32[1,128,128]{1,2,0:T(8,128)S(1)}, f32[1,128,128]{1,2,0:T(8,128)S(1)}, u32[]{:S(2)}, u32[]{:S(2)}) collective-permute-start(f32[1,128,128]{1,2,0:T(8,128)S(1)} %bitcast.120), channel_id=1, source_target_pairs={{1,0},{2,1},{3,2},{4,3},{5,4},{6,5},{7,6},{0,7},{9,8},{10,9},{11,1... | collective-permute-start | bytes 196616 | tf_op jit(solution)/shard_map/ppermute | solution.py:18
  32.0 2.5 %collective-permute-done.4 = f32[1,128,128]{1,2,0:T(8,128)S(1)} collective-permute-done((f32[1,128,128]{1,2,0:T(8,128)S(1)}, f32[1,128,128]{1,2,0:T(8,128)S(1)}, u32[]{:S(2)}, u32[]{:S(2)}) %collective-permute-start.4) | collective-permute-done | bytes 65568 | tf_op jit(solution)/shard_map/ppermute | solution.py:16
  34.6 2.5 %scatter_custom_fusion = f32[769,128]{1,0:T(8,128)S(1)} fusion(s32[384]{0:T(512)S(1)} %fusion.45, f32[384,128]{1,0:T(8,128)S(1)} %bitcast.122, f32[]{:T(128)} %constant.134.clone.1), kind=kCustom, calls=%fused_computation.32 | custom fusion | flops 49152 | bytes 393732 | tf_op jit(solution)/shard_map/scatter-add | solution.py:84
  37.3 5.6 %all_gather.22 = bf16[768,128]{1,0:T(8,128)(2,1)S(1)} all-gather(bf16[192,128]{1,0:T(8,128)(2,1)S(1)} %fusion.6), channel_id=1, replica_groups=mesh['sec'=4,'sub'=8] {'sec'}, dimensions={0}, use_global_device_ids=true | all-gather | bytes 245760 | tf_op jit(solution)/shard_map/all_gather | solution.py:90
  42.9 4.7 %collective-permute-start.7 = (bf16[768,128]{1,0:T(8,128)(2,1)S(1)}, bf16[768,128]{1,0:T(8,128)(2,1)S(1)}, u32[]{:S(2)}, u32[]{:S(2)}) collective-permute-start(bf16[768,128]{1,0:T(8,128)(2,1)S(1)} %all_gather.22), channel_id=1, source_target_pairs={{1,0},{2,1},{3,2},{4,3},{5,4},{6,5},{7,6},{0,7},{9,8},{10,9},{11,1... | collective-permute-start | bytes 589832 | tf_op jit(solution)/shard_map/ppermute | solution.py:18
  47.6 5.8 %all_gather.19 = bf16[1,1024,128]{2,1,0:T(8,128)(2,1)S(1)} all-gather(bf16[1,256,128]{2,1,0:T(8,128)(2,1)S(1)} %fusion.4), channel_id=1, replica_groups=mesh['sec'=4,'sub'=8] {'sec'}, dimensions={1}, use_global_device_ids=true | all-gather | bytes 327680 | tf_op jit(solution)/shard_map/all_gather | solution.py:95
  53.4 0.9 %collective-permute-done.7 = bf16[768,128]{1,0:T(8,128)(2,1)S(1)} collective-permute-done((bf16[768,128]{1,0:T(8,128)(2,1)S(1)}, bf16[768,128]{1,0:T(8,128)(2,1)S(1)}, u32[]{:S(2)}, u32[]{:S(2)}) %collective-permute-start.7) | collective-permute-done | bytes 196640 | tf_op jit(solution)/shard_map/ppermute | solution.py:18
  54.3 0.7 gather_fusion
  55.3 0.3 convolution_add_fusion
  55.6 0.3 collective-permute-start.8
  56.0 4.4 %collective-permute-start.9 = (f32[1,256,128]{1,2,0:T(8,128)S(1)}, f32[1,256,128]{1,2,0:T(8,128)S(1)}, u32[]{:S(2)}, u32[]{:S(2)}) collective-permute-start(f32[1,256,128]{1,2,0:T(8,128)S(1)} %bitcast.116), channel_id=1, source_target_pairs={{1,0},{2,1},{3,2},{4,3},{5,4},{6,5},{7,6},{0,7},{9,8},{10,9},{11,1... | collective-permute-start | bytes 393224 | tf_op jit(solution)/shard_map/ppermute | solution.py:18
  60.4 3.0 %collective-permute-done.8 = f32[1,256,128]{1,2,0:T(8,128)S(1)} collective-permute-done((f32[1,256,128]{1,2,0:T(8,128)S(1)}, f32[1,256,128]{1,2,0:T(8,128)S(1)}, u32[]{:S(2)}, u32[]{:S(2)}) %collective-permute-start.8) | collective-permute-done | bytes 131104 | tf_op jit(solution)/shard_map/ppermute | solution.py:16
  63.7 0.4 fusion.3
  64.1 5.8 %all-gather.1 = bf16[1024,128]{0,1:T(8,128)(2,1)S(1)} all-gather(bf16[256,128]{0,1:T(8,128)(2,1)S(1)} %fusion.3), channel_id=3, replica_groups=mesh['sec'=4,'sub'=8] {'sec'}, dimensions={0}, use_global_device_ids=true | all-gather | bytes 327680 | tf_op jit(solution)/shard_map/all_gather | solution.py:103
  69.9 0.3 fusion.5
  70.2 0.7 %copy.23 = bf16[1,256,128]{2,1,0:T(8,128)(2,1)} copy(bf16[1,256,128]{1,2,0:T(8,128)(2,1)S(1)} %fusion.5) | data formatting | bytes 131072
  71.0 0.7 %copy.22 = bf16[1,256,128]{2,1,0:T(8,128)(2,1)} copy(bf16[1,256,128]{1,2,0:T(8,128)(2,1)S(1)} %bitcast.118) | data formatting | bytes 131072
  (39 shorter events, 2.1 us)
Async XLA Ops:
  0.6 7.6 %copy-start = (bf16[1,256,1024]{2,1,0:T(8,128)(2,1)S(1)}, bf16[1,256,1024]{2,1,0:T(8,128)(2,1)}, u32[]{:S(2)}) copy-start(bf16[1,256,1024]{2,1,0:T(8,128)(2,1)} %param.11) | copy-start | bytes 1572868
  0.6 13.5 %copy-start.4 = (s32[1,128]{1,0:T(1,128)S(1)}, s32[1,128]{1,0:T(1,128)}, u32[]{:S(2)}) copy-start(s32[1,128]{1,0:T(1,128)} %param.19) | copy-start | bytes 1540
  0.7 18.3 %copy-start.6 = (s32[1,4]{1,0:T(1,128)S(1)}, s32[1,4]{1,0:T(1,128)}, u32[]{:S(2)}) copy-start(s32[1,4]{1,0:T(1,128)} %param.17) | copy-start | bytes 52
  8.2 12.3 %copy-start.5 = (s32[1,256]{1,0:T(1,128)S(1)}, s32[1,256]{1,0:T(1,128)}, u32[]{:S(2)}) copy-start(s32[1,256]{1,0:T(1,128)} %param.18) | copy-start | bytes 3076
  8.2 12.6 %copy-start.3 = (bf16[1,256,128]{2,1,0:T(8,128)(2,1)S(1)}, bf16[1,256,128]{2,1,0:T(8,128)(2,1)}, u32[]{:S(2)}) copy-start(bf16[1,256,128]{2,1,0:T(8,128)(2,1)} %param.13) | copy-start | bytes 196612
  9.4 11.1 %collective-permute-start = (f32[1,256,128]{2,1,0:T(8,128)S(1)}, f32[1,256,128]{2,1,0:T(8,128)S(1)}, u32[]{:S(2)}, u32[]{:S(2)}) collective-permute-start(f32[1,256,128]{2,1,0:T(8,128)S(1)} %fusion.2), channel_id=1, source_target_pairs={{0,1},{1,2},{2,3},{3,4},{4,5},{5,6},{6,7},{7,0},{8,9},{9,10},{10,1... | collective-permute-start | bytes 393224 | tf_op jit(solution)/shard_map/ppermute | solution.py:16
  11.0 9.5 %collective-permute-start.1 = (f32[1,256,128]{2,1,0:T(8,128)S(1)}, f32[1,256,128]{2,1,0:T(8,128)S(1)}, u32[]{:S(2)}, u32[]{:S(2)}) collective-permute-start(f32[1,256,128]{2,1,0:T(8,128)S(1)} %fusion.2), channel_id=1, source_target_pairs={{1,0},{2,1},{3,2},{4,3},{5,4},{6,5},{7,6},{0,7},{9,8},{10,9},{11,1... | collective-permute-start | bytes 393224 | tf_op jit(solution)/shard_map/ppermute | solution.py:18
  14.2 6.3 %collective-permute-start.2 = (s32[1,128]{1,0:T(1,128)S(1)}, s32[1,128]{1,0:T(1,128)S(1)}, u32[]{:S(2)}, u32[]{:S(2)}) collective-permute-start(s32[1,128]{1,0:T(1,128)S(1)} %copy-done.4), channel_id=1, source_target_pairs={{0,1},{1,2},{2,3},{3,4},{4,5},{5,6},{6,7},{7,0},{8,9},{9,10},{10,1... | collective-permute-start | bytes 1544 | tf_op jit(solution)/shard_map/ppermute | solution.py:16
  14.2 6.3 %collective-permute-start.3 = (s32[1,128]{1,0:T(1,128)S(1)}, s32[1,128]{1,0:T(1,128)S(1)}, u32[]{:S(2)}, u32[]{:S(2)}) collective-permute-start(s32[1,128]{1,0:T(1,128)S(1)} %copy-done.4), channel_id=1, source_target_pairs={{1,0},{2,1},{3,2},{4,3},{5,4},{6,5},{7,6},{0,7},{9,8},{10,9},{11,1... | collective-permute-start | bytes 1544 | tf_op jit(solution)/shard_map/ppermute | solution.py:18
  27.1 7.4 %collective-permute-start.4 = (f32[1,128,128]{1,2,0:T(8,128)S(1)}, f32[1,128,128]{1,2,0:T(8,128)S(1)}, u32[]{:S(2)}, u32[]{:S(2)}) collective-permute-start(f32[1,128,128]{1,2,0:T(8,128)S(1)} %bitcast.119), channel_id=1, source_target_pairs={{0,1},{1,2},{2,3},{3,4},{4,5},{5,6},{6,7},{7,0},{8,9},{9,10},{10,1... | collective-permute-start | bytes 196616 | tf_op jit(solution)/shard_map/ppermute | solution.py:16
  27.1 7.3 %collective-permute-start.5 = (f32[1,128,128]{1,2,0:T(8,128)S(1)}, f32[1,128,128]{1,2,0:T(8,128)S(1)}, u32[]{:S(2)}, u32[]{:S(2)}) collective-permute-start(f32[1,128,128]{1,2,0:T(8,128)S(1)} %bitcast.120), channel_id=1, source_target_pairs={{1,0},{2,1},{3,2},{4,3},{5,4},{6,5},{7,6},{0,7},{9,8},{10,9},{11,1... | collective-permute-start | bytes 196616 | tf_op jit(solution)/shard_map/ppermute | solution.py:18
  31.9 5.1 %copy-start.2 = (bf16[1,192,768]{2,1,0:T(8,128)(2,1)S(1)}, bf16[1,192,768]{2,1,0:T(8,128)(2,1)}, u32[]{:S(2)}) copy-start(bf16[1,192,768]{2,1,0:T(8,128)(2,1)} %param.14) | copy-start | bytes 884740
  42.9 10.5 %collective-permute-start.6 = (bf16[768,128]{1,0:T(8,128)(2,1)S(1)}, bf16[768,128]{1,0:T(8,128)(2,1)S(1)}, u32[]{:S(2)}, u32[]{:S(2)}) collective-permute-start(bf16[768,128]{1,0:T(8,128)(2,1)S(1)} %all_gather.22), channel_id=1, source_target_pairs={{0,1},{1,2},{2,3},{3,4},{4,5},{5,6},{6,7},{7,0},{8,9},{9,10},{10,1... | collective-permute-start | bytes 589832 | tf_op jit(solution)/shard_map/ppermute | solution.py:16
  42.9 11.4 %collective-permute-start.7 = (bf16[768,128]{1,0:T(8,128)(2,1)S(1)}, bf16[768,128]{1,0:T(8,128)(2,1)S(1)}, u32[]{:S(2)}, u32[]{:S(2)}) collective-permute-start(bf16[768,128]{1,0:T(8,128)(2,1)S(1)} %all_gather.22), channel_id=1, source_target_pairs={{1,0},{2,1},{3,2},{4,3},{5,4},{6,5},{7,6},{0,7},{9,8},{10,9},{11,1... | collective-permute-start | bytes 589832 | tf_op jit(solution)/shard_map/ppermute | solution.py:18
  53.4 1.9 %copy-start.1 = (bf16[1,256,1024]{2,1,0:T(8,128)(2,1)S(1)}, bf16[1,256,1024]{2,1,0:T(8,128)(2,1)}, u32[]{:S(2)}) copy-start(bf16[1,256,1024]{2,1,0:T(8,128)(2,1)} %param.12) | copy-start | bytes 1572868
  55.6 7.8 %collective-permute-start.8 = (f32[1,256,128]{1,2,0:T(8,128)S(1)}, f32[1,256,128]{1,2,0:T(8,128)S(1)}, u32[]{:S(2)}, u32[]{:S(2)}) collective-permute-start(f32[1,256,128]{1,2,0:T(8,128)S(1)} %bitcast.115), channel_id=1, source_target_pairs={{0,1},{1,2},{2,3},{3,4},{4,5},{5,6},{6,7},{7,0},{8,9},{9,10},{10,1... | collective-permute-start | bytes 393224 | tf_op jit(solution)/shard_map/ppermute | solution.py:16
  56.0 7.8 %collective-permute-start.9 = (f32[1,256,128]{1,2,0:T(8,128)S(1)}, f32[1,256,128]{1,2,0:T(8,128)S(1)}, u32[]{:S(2)}, u32[]{:S(2)}) collective-permute-start(f32[1,256,128]{1,2,0:T(8,128)S(1)} %bitcast.116), channel_id=1, source_target_pairs={{1,0},{2,1},{3,2},{4,3},{5,4},{6,5},{7,6},{0,7},{9,8},{10,9},{11,1... | collective-permute-start | bytes 393224 | tf_op jit(solution)/shard_map/ppermute | solution.py:18
